TPU v7x, 32 devices: a whole 2x2x4 slice. The times are simulated.
32 devices in a mesh: row: 4 (over z), col: 8 (over y, x, core).
Axes of the slice: x: 2, y: 2, z: 4, core: 2. Of those that a mesh axis runs over, the one named last changes fastest.
Arguments:
- occupations: int32 [4096, 128], P('row'), may hold values from 0 to 2
- table: float32 [384, 1024], replicated, may hold values from -0.5 to 0.5
- weights: float32 [2, 1024, 4096], P(None, None, 'col'), may hold values from -0.1875 to 0.1875
- biases: float32 [2, 4096], P(None, 'col'), may hold values from -6 to 6
- heads: float32 [2, 4096], P(None, 'col'), may hold values from -18 to 18
- energies: float32 [4096], P('row'), may hold values from -6 to 6
Outputs:
- schur: float32 [4096, 4096], P('row', 'col')
- solved_rhs: float32 [4096], P('row')
All inputs are finite; a program needn't handle non-finite values.
Results may differ from a plain program's by a relative error of at most 0.0034.
Values may be sent and summed in bfloat16 or wider, within the bound.
A program may use at most 128 MiB of HBM per device.

v0:
```python
import math
import jax
import jax.numpy as jnp
from jax import lax
from jax.sharding import PartitionSpec as P

norm_eps = 1e-06
diag_shift = 0.05


def broadcast(block, axis, holder):
    block = jnp.where(lax.axis_index(axis) == holder, block, jnp.zeros_like(block))
    return lax.psum(block, axis)


def jacobian(occupations, table, weights, biases, heads):
    onehot = jnp.concatenate(
        [
            (occupations == 0).astype(jnp.float32),
            (occupations == 1).astype(jnp.float32),
            (occupations == 2).astype(jnp.float32),
        ],
        axis=1,
    )
    embedded = jnp.dot(
        onehot, table, precision=lax.Precision.HIGHEST, preferred_element_type=jnp.float32
    )
    embedded = embedded * lax.rsqrt(
        jnp.mean(embedded * embedded, axis=-1, keepdims=True) + norm_eps
    )
    blocks = []
    for panel_index in range(2):
        hidden = (
            jnp.dot(
                embedded,
                weights[panel_index],
                precision=lax.Precision.HIGHEST,
                preferred_element_type=jnp.float32,
            )
            + biases[panel_index]
        )
        blocks.append(heads[panel_index] * jax.nn.sigmoid(hidden))
    return jnp.concatenate(blocks, axis=1)


def on_device(occupations, table, weights, biases, heads, energies):
    row_count = occupations.shape[0]
    row_devices = lax.axis_size("row")
    col_devices = lax.axis_size("col")
    sample_total = row_count * row_devices
    panel_width = sample_total // col_devices
    derivs = jacobian(occupations, table, weights, biases, heads)
    col_sums = lax.psum(jnp.sum(derivs, axis=0), "row")
    centered = ((derivs - col_sums / sample_total) * (1.0 / math.sqrt(sample_total))).astype(
        jnp.bfloat16
    )
    own_rows = lax.all_gather(centered, "col", axis=1, tiled=True)
    every_sample = lax.all_gather(centered, "row", axis=0, tiled=True)
    partner = lax.all_to_all(every_sample, "col", split_axis=0, concat_axis=1, tiled=True)
    kernel = lax.dot_general(
        own_rows, partner, (((1,), (1,)), ((), ())), preferred_element_type=jnp.float32
    )
    row_ids = lax.axis_index("row") * row_count + lax.iota(jnp.int32, row_count)
    col_ids = lax.axis_index("col") * panel_width + lax.iota(jnp.int32, panel_width)
    kernel = kernel + jnp.where(row_ids[:, None] == col_ids[None, :], diag_shift, 0.0).astype(
        jnp.float32
    )
    right_side = energies
    for panel_index in range(2):
        start_global = panel_index * panel_width
        root_row = start_global // row_count
        offset = start_global % row_count
        top_block, top_side = (
            broadcast(kernel[offset : offset + panel_width], "row", root_row),
            broadcast(right_side[offset : offset + panel_width], "row", root_row),
        )
        column, diag_block = (
            broadcast(kernel, "col", panel_index),
            broadcast(top_block, "col", panel_index),
        )
        factor = jnp.linalg.cholesky(diag_block)
        left_rows = lax.linalg.triangular_solve(
            factor, column, left_side=False, lower=True, transpose_a=True
        )
        right_rows = lax.linalg.triangular_solve(
            factor, top_block.T, left_side=False, lower=True, transpose_a=True
        )
        kernel = kernel - lax.dot_general(
            left_rows,
            right_rows,
            (((1,), (1,)), ((), ())),
            precision=lax.Precision.HIGHEST,
            preferred_element_type=jnp.float32,
        )
        solved = lax.linalg.triangular_solve(factor, top_side[:, None], left_side=True, lower=True)[
            :, 0
        ]
        right_side = right_side - jnp.dot(
            left_rows, solved, precision=lax.Precision.HIGHEST, preferred_element_type=jnp.float32
        )
        placed = right_side.at[offset : offset + panel_width].set(solved)
        right_side = jnp.where(lax.axis_index("row") == root_row, placed, right_side)
    return (kernel, right_side)


def solution(mesh):
    placed = (P("row", None), P(), P(None, None, "col"), P(None, "col"), P(None, "col"), P("row"))
    return jax.shard_map(
        on_device,
        mesh=mesh,
        in_specs=placed,
        out_specs=(P("row", "col"), P("row")),
        check_vma=False,
    )
```

profile of v0, /device:TPU:0, one launch (start us, length us, event | category | flops | bytes accessed | tf_op | source)
XLA Modules:
  0.0 969.1 jit_solution(3831402307478594253)
XLA Ops:
  7.2 1.4 broadcast_compare_fusion.2
  8.7 5.1 multiply_reduce_fusion
  13.9 12.5 %divide_multiply_fusion.1 = f32[1024,512]{0,1:T(8,128)S(1)} fusion(f32[2,1024,512]{2,1,0:T(8,128)} %param.19, f32[1024,1024]{0,1:T(8,128)} %get-tuple-element.136, f32[1024]{0:T(1024)S(1)} %add_rsqrt_fusion, f32[512]{0:T(512)S(1)} %bitcast.291, f32[512]{0:T(512)S(1)} %bitcast.290), kind=kOutput, calls=%fused_computation.20 | convolution fusion | flops 6446120960 | bytes 8396800 | tf_op jit(solution)/shard_map/dot_general | solution.py:34
  26.4 7.2 divide_multiply_fusion
  33.6 1.3 copy-done.5
  35.6 13.7 %all-reduce.3 = (f32[1024]{0:T(1024)S(1)}, f32[512,1]{0,1:T(1,128)S(1)}) all-reduce(f32[1024]{0:T(1024)S(1)} %fusion.4, f32[512,1]{0,1:T(1,128)S(1)} %bitcast.282), channel_id=1, replica_groups=mesh['row'=4,'col'=8] {'row'}, use_global_device_ids=true, to_apply=%region_2.0 | all-reduce | flops 1536 | bytes 12288 | tf_op jit(solution)/shard_map/psum | solution.py:53
  49.4 3.9 multiply_convert_fusion
  54.1 147.2 %all-gather.5.cloned.1.call-done = bf16[4096,1024]{0,1:T(8,128)(2,1)} async-done(((bf16[1024,1024]{0,1:T(8,128)(2,1)}), bf16[4096,1024]{0,1:T(8,128)(2,1)}) %all-gather.5.cloned.1.call-update) | async-done | bytes 8388624 | tf_op jit(solution)/shard_map/all_gather | solution.py:58
  201.3 7.9 copy.26
  209.1 5.0 all-to-all-start
  214.2 126.8 %all-to-all-done = bf16[8,512,1024]{1,2,0:T(8,128)(2,1)} async-done(((bf16[8,512,1024]{1,2,0:T(8,128)(2,1)}), bf16[8,512,1024]{1,2,0:T(8,128)(2,1)}, u32[]{:S(2)}, u32[]{:S(2)}) %all-to-all-start) | async-done | bytes 8388640 | tf_op jit(solution)/shard_map/all_to_all | solution.py:59
  341.0 32.8 %all-gather.3.cloned.1.call-done = bf16[1024,8192]{0,1:T(8,128)(2,1)} async-done(((bf16[1024,1024]{0,1:T(8,128)(2,1)}), bf16[1024,8192]{0,1:T(8,128)(2,1)}) %all-gather.3.cloned.1.call-update) | async-done | bytes 16777232 | tf_op jit(solution)/shard_map/all_gather | solution.py:57
  373.8 15.9 %broadcast_select_fusion.1 = (f32[1024,512]{0,1:T(8,128)}, f32[1024,512]{0,1:T(8,128)S(1)}) fusion(pred[]{:T(512)S(6)} %eq.56, s32[512]{0:T(512)S(1)} %iota_add_fusion.1, s32[1024]{0:T(1024)S(1)} %iota_add_fusion, bf16[1024,8192]{0,1:T(8,128)(2,1)} %all-gather.3.cloned.1.call-done, bf16[512,8192]{0,1:T(8,128)(2,1)} %bitcast.7), kind=kOutput, calls=%fused_computation.118 | convolution fusion | flops 8592031744 | bytes 29366272 | tf_op jit(solution)/shard_map/dot_general | solution.py:60
  389.7 1.3 copy-done.6
  392.2 51.6 %all-reduce.9.cloned.1.call-done = f32[512,512]{0,1:T(8,128)} async-done(((f32[512,512]{0,1:T(8,128)}), f32[512,512]{0,1:T(8,128)}) %all-reduce.9.cloned.1.call-update) | async-done | bytes 1048592 | tf_op jit(solution)/shard_map/psum | solution.py:13
  443.8 2.3 broadcast_select_fusion.3
  446.6 69.6 %all-reduce.15.cloned.1.call-done = (f32[1024,512]{0,1:T(8,128)}, f32[512,512]{0,1:T(8,128)}) async-done(((f32[1024,512]{0,1:T(8,128)}, f32[512,512]{0,1:T(8,128)}), (f32[1024,512]{0,1:T(8,128)}, f32[512,512]{0,1:T(8,128)})) %all-reduce.15.cloned.1.call-update) | async-done | bytes 3145744 | tf_op jit(solution)/shard_map/psum | solution.py:13
  516.2 1.6 copy.16
  519.1 11.7 %cholesky.286 = f32[128,128]{1,0:T(8,128)S(1)} custom-call(f32[128,128]{1,0:T(8,128)S(1)} %cholesky.426), custom_call_target="Cholesky" | custom-call | tf_op jit(solution)/shard_map/jit(cholesky)/cholesky | solution.py:81
  531.0 9.8 %custom-call.35 = f32[1,128,128]{1,2,0:T(8,128)S(1)} custom-call(f32[1,128,128]{2,1,0:T(8,128)S(1)} %get-tuple-element.130), custom_call_target="InvertDiagBlocksLowerTriangular" | custom-call | tf_op jit(solution)/shard_map/jit(cholesky)/cholesky | solution.py:81
  542.0 1.3 convolution_subtract_fusion.13
  543.3 11.7 %cholesky.305 = f32[128,128]{1,0:T(8,128)S(1)} custom-call(f32[128,128]{1,0:T(8,128)S(1)} %cholesky.430), custom_call_target="Cholesky" | custom-call | tf_op jit(solution)/shard_map/jit(cholesky)/cholesky | solution.py:81
  555.1 10.0 %custom-call.36 = f32[1,128,128]{1,2,0:T(8,128)S(1)} custom-call(f32[1,128,128]{2,1,0:T(8,128)S(1)} %get-tuple-element.127), custom_call_target="InvertDiagBlocksLowerTriangular" | custom-call | tf_op jit(solution)/shard_map/jit(cholesky)/cholesky | solution.py:81
  565.3 1.3 convolution_subtract_fusion.15
  566.6 11.7 %cholesky.326 = f32[128,128]{1,0:T(8,128)S(1)} custom-call(f32[128,128]{1,0:T(8,128)S(1)} %cholesky.435), custom_call_target="Cholesky" | custom-call | tf_op jit(solution)/shard_map/jit(cholesky)/cholesky | solution.py:81
  579.0 9.8 %custom-call.37 = f32[1,128,128]{1,2,0:T(8,128)S(1)} custom-call(f32[1,128,128]{2,1,0:T(8,128)S(1)} %get-tuple-element.124), custom_call_target="InvertDiagBlocksLowerTriangular" | custom-call | tf_op jit(solution)/shard_map/jit(cholesky)/cholesky | solution.py:81
  590.3 11.7 %cholesky.343 = f32[128,128]{1,0:T(8,128)S(1)} custom-call(f32[128,128]{1,0:T(8,128)S(1)} %convolution_subtract_fusion.17), custom_call_target="Cholesky" | custom-call | tf_op jit(solution)/shard_map/jit(cholesky)/cholesky | solution.py:81
  606.6 8.0 while.14
  607.3 1.4 bitcast_dynamic-update-slice_fusion.4
  609.3 1.4 bitcast_dynamic-update-slice_fusion.4
  611.3 1.4 bitcast_dynamic-update-slice_fusion.4
  613.3 1.4 bitcast_dynamic-update-slice_fusion.4
  614.7 39.3 %custom-call.38 = f32[4,128,128]{1,2,0:T(8,128)S(1)} custom-call(f32[4,128,128]{2,1,0:T(8,128)S(1)} %get-tuple-element.72), custom_call_target="InvertDiagBlocksLowerTriangular" | custom-call | tf_op jit(solution)/shard_map/triangular_solve/custom-call.3 | solution.py:82
  654.0 1.7 fusion.85
  655.7 1.6 convolution_subtract_fusion.5
  657.9 1.8 convolution_subtract_fusion.3
  660.3 2.3 fusion.32
  666.2 1.5 convolution_subtract_fusion.11
  668.1 5.1 broadcast_select_fusion
  673.2 1.3 copy-done.2
  676.3 51.5 %all-reduce.11.cloned.1.call-done = f32[512,512]{0,1:T(8,128)} async-done(((f32[512,512]{0,1:T(8,128)}), f32[512,512]{0,1:T(8,128)}) %all-reduce.11.cloned.1.call-update) | async-done | bytes 1048592 | tf_op jit(solution)/shard_map/psum | solution.py:13
  731.1 10.1 %psum.71 = f32[512,1]{0,1:T(1,128)S(1)} all-reduce(f32[512,1]{0,1:T(1,128)S(1)} %bitcast.285), channel_id=1, replica_groups=mesh['row'=4,'col'=8] {'row'}, use_global_device_ids=true, to_apply=%region_18.23 | all-reduce | flops 512 | bytes 4096 | tf_op jit(solution)/shard_map/psum | solution.py:13
  741.3 58.9 %all-reduce.13.cloned.1.call-done = (f32[1024,512]{0,1:T(8,128)}, f32[512,512]{0,1:T(8,128)}) async-done(((f32[1024,512]{0,1:T(8,128)}, f32[512,512]{0,1:T(8,128)}), (f32[1024,512]{0,1:T(8,128)}, f32[512,512]{0,1:T(8,128)})) %all-reduce.13.cloned.1.call-update) | async-done | bytes 3145744 | tf_op jit(solution)/shard_map/psum | solution.py:13
  800.2 1.6 copy.18
  803.1 11.7 %cholesky.358 = f32[128,128]{1,0:T(8,128)S(1)} custom-call(f32[128,128]{1,0:T(8,128)S(1)} %cholesky.439), custom_call_target="Cholesky" | custom-call | tf_op jit(solution)/shard_map/jit(cholesky)/cholesky | solution.py:81
  815.0 9.8 %custom-call.40 = f32[1,128,128]{1,2,0:T(8,128)S(1)} custom-call(f32[1,128,128]{2,1,0:T(8,128)S(1)} %get-tuple-element.120), custom_call_target="InvertDiagBlocksLowerTriangular" | custom-call | tf_op jit(solution)/shard_map/jit(cholesky)/cholesky | solution.py:81
  826.0 1.3 convolution_subtract_fusion.12
  827.3 11.7 %cholesky.377 = f32[128,128]{1,0:T(8,128)S(1)} custom-call(f32[128,128]{1,0:T(8,128)S(1)} %cholesky.443), custom_call_target="Cholesky" | custom-call | tf_op jit(solution)/shard_map/jit(cholesky)/cholesky | solution.py:81
  840.4 10.2 %custom-call.41 = f32[1,128,128]{1,2,0:T(8,128)S(1)} custom-call(f32[1,128,128]{2,1,0:T(8,128)S(1)} %get-tuple-element.117), custom_call_target="InvertDiagBlocksLowerTriangular" | custom-call | tf_op jit(solution)/shard_map/jit(cholesky)/cholesky | solution.py:81
  850.9 1.3 convolution_subtract_fusion.14
  852.2 11.7 %cholesky.398 = f32[128,128]{1,0:T(8,128)S(1)} custom-call(f32[128,128]{1,0:T(8,128)S(1)} %cholesky.448), custom_call_target="Cholesky" | custom-call | tf_op jit(solution)/shard_map/jit(cholesky)/cholesky | solution.py:81
  864.7 9.8 %custom-call.42 = f32[1,128,128]{1,2,0:T(8,128)S(1)} custom-call(f32[1,128,128]{2,1,0:T(8,128)S(1)} %get-tuple-element.114), custom_call_target="InvertDiagBlocksLowerTriangular" | custom-call | tf_op jit(solution)/shard_map/jit(cholesky)/cholesky | solution.py:81
  875.9 11.7 %cholesky.415 = f32[128,128]{1,0:T(8,128)S(1)} custom-call(f32[128,128]{1,0:T(8,128)S(1)} %convolution_subtract_fusion.16), custom_call_target="Cholesky" | custom-call | tf_op jit(solution)/shard_map/jit(cholesky)/cholesky | solution.py:81
  891.3 8.0 while.15
  891.9 1.4 bitcast_dynamic-update-slice_fusion.5
  893.9 1.4 bitcast_dynamic-update-slice_fusion.5
  895.9 1.4 bitcast_dynamic-update-slice_fusion.5
  897.9 1.4 bitcast_dynamic-update-slice_fusion.5
  899.3 39.3 %custom-call.43 = f32[4,128,128]{1,2,0:T(8,128)S(1)} custom-call(f32[4,128,128]{2,1,0:T(8,128)S(1)} %get-tuple-element.74), custom_call_target="InvertDiagBlocksLowerTriangular" | custom-call | tf_op jit(solution)/shard_map/triangular_solve/custom-call.3 | solution.py:82
  940.1 1.7 fusion.83
  941.8 1.6 convolution_subtract_fusion.4
  951.3 1.5 convolution_subtract_fusion.10
  953.3 5.2 convolution_subtract_fusion
  958.5 2.9 copy.20
  (164 shorter events, 43.2 us)
Async XLA Ops:
  7.2 1.6 copy-start
  7.2 194.1 %all-gather.5.cloned.1.call-start = ((), (), s32[]{:S(2)}) async-start(), calls=%async_computation.2 | async-start | bytes 10485760 | tf_op jit(solution)/shard_map/all_gather | solution.py:58
  8.7 5.1 copy-start.19
  8.7 5.1 copy-start.20
  13.8 12.6 %copy-start.21 = (f32[2,1024,512]{2,1,0:T(8,128)S(1)}, f32[2,1024,512]{2,1,0:T(8,128)}, u32[]{:S(2)}) copy-start(f32[2,1024,512]{2,1,0:T(8,128)} %param.19) | copy-start | bytes 12582916
  13.9 12.6 %copy-start.22 = (f32[1024,1024]{0,1:T(8,128)S(1)}, f32[1024,1024]{0,1:T(8,128)}, u32[]{:S(2)}) copy-start(f32[1024,1024]{0,1:T(8,128)} %get-tuple-element.136) | copy-start | bytes 12582916
  26.4 7.2 copy-start.4
  33.6 1.3 copy-start.5
  34.9 0.7 copy-start.17
  53.3 320.5 %all-gather.3.cloned.1.call-start = ((), (), s32[]{:S(2)}) async-start(), calls=%async_computation.1 | async-start | bytes 18874368 | tf_op jit(solution)/shard_map/all_gather | solution.py:57
  209.1 131.9 %all-to-all-start = ((bf16[8,512,1024]{1,2,0:T(8,128)(2,1)}), bf16[8,512,1024]{1,2,0:T(8,128)(2,1)}, u32[]{:S(2)}, u32[]{:S(2)}) async-start(bf16[8,512,1024]{1,2,0:T(8,128)(2,1)} %bitcast.258), calls=%async_computation | async-start | bytes 16777216 | tf_op jit(solution)/shard_map/all_to_all | solution.py:59
  214.1 229.6 %all-reduce.9.cloned.1.call-start = ((), (), s32[]{:S(2)}) async-start(), calls=%async_computation.3 | async-start | bytes 2097152 | tf_op jit(solution)/shard_map/psum | solution.py:13
  389.7 1.4 copy-start.6
  392.2 124.1 %all-reduce.15.cloned.1.call-start = ((), (), s32[]{:S(2)}) async-start(), calls=%async_computation.6 | async-start | bytes 6291456 | tf_op jit(solution)/shard_map/psum | solution.py:13
  446.1 281.7 %all-reduce.11.cloned.1.call-start = ((), (), s32[]{:S(2)}) async-start(), calls=%async_computation.4 | async-start | bytes 2097152 | tf_op jit(solution)/shard_map/psum | solution.py:13
  516.2 1.7 copy-start.9
  518.1 1.0 copy-start.13
  660.3 2.9 copy-start.11
  663.3 4.8 copy-start.14
  664.3 3.7 copy-start.7
  673.2 1.4 copy-start.2
  675.7 124.5 %all-reduce.13.cloned.1.call-start = ((), (), s32[]{:S(2)}) async-start(), calls=%async_computation.5 | async-start | bytes 6291456 | tf_op jit(solution)/shard_map/psum | solution.py:13
  728.9 1.0 copy-start.15
  800.2 1.7 copy-start.8
  802.1 1.0 copy-start.12
  939.4 4.7 copy-start.16
  946.6 1.8 copy-start.10
  949.5 3.8 copy-start.3
  953.3 8.7 copy-start.1
  961.4 0.6 copy-start.18
Sparse Core Ops, SparseCore 0:
  53.5 147.7 all-gather.4
  203.1 170.6 all-gather.2
  392.3 51.4 all-reduce.8
  447.6 68.6 all-reduce.14
  675.8 51.9 all-reduce.10
  731.6 68.6 all-reduce.12
where the time goes:
time: 975 us; the launch traced here: 969 us
  waiting for transfers between devices  539 us (55%)
  other arithmetic  249 us (26%)
  matrix products  92.9 us (10%)
  local copies, waits for them, and re-layouts  37.6 us (4%)
  blocking collectives  23.8 us (2%)
  between operations  20.4 us (2%)
    psum x4, waiting for transfers between devices, broadcast(): return lax.psum(block, axis)  232 us
    another operation x29, other arithmetic, on_device(): factor = jnp.linalg.cholesky(diag_block)  158 us
    all_gather x1, waiting for transfers between devices, on_device(): every_sample = lax.all_gather(centered, 'row', axis=0, tiled=True)  147 us
    all_to_all x1, waiting for transfers between devices, on_device(): lax.all_to_all(every_sample, 'col', split_axis=0, concat_axis=1, tiled=True)  127 us
    another operation x5, other arithmetic, on_device(): lax.linalg.triangular_solve(factor, column, left_side=False, lower=True,...  79.4 us
    all_gather x1, waiting for transfers between devices, on_device(): own_rows = lax.all_gather(centered, 'col', axis=1, tiled=True)  32.8 us
    dot_general x2, matrix products, jacobian(): jnp.dot(embedded, weights[panel_index], precision=lax.Precision.HIGHEST,...  19.7 us
  transfers between devices with their start and end apart: 7, of which 7 were waited for; matrix products, arithmetic and copies ran while one was open for 1% of the time, Pallas kernels for 0%

commit v1 on v0

--- a/solution.py
+++ b/solution.py
@@ -55,7 +55,18 @@
         jnp.bfloat16
     )
     own_rows = lax.all_gather(centered, "col", axis=1, tiled=True)
-    every_sample = lax.all_gather(centered, "row", axis=0, tiled=True)
+    by_rank = [centered]
+    how_many = lax.psum(1, axis_name="row")
+    for nth in [*range(how_many - 1)]:
+        by_rank.append(
+            lax.ppermute(
+                by_rank[-1],
+                axis_name="row",
+                perm=[(w, (w + 1) % how_many) for w in range(how_many)],
+            )
+        )
+    s_next = jnp.concatenate(by_rank[::-1], axis=0)
+    every_sample = jnp.roll(s_next, (lax.axis_index("row") + 1) * centered.shape[0], axis=0)
     partner = lax.all_to_all(every_sample, "col", split_axis=0, concat_axis=1, tiled=True)
     kernel = lax.dot_general(
         own_rows, partner, (((1,), (1,)), ((), ())), preferred_element_type=jnp.float32

time: 975 us -> 943 us (0.967)
  waiting for transfers between devices: 539 us -> 462 us
  local copies, waits for them, and re-layouts: 37.6 us -> 82 us
    all_gather x1 -> x0, waiting for transfers between devices: 147 us -> none  [on_device(): every_sample = lax.all_gather(centered, 'row', axis=0, tiled=True)]
    ppermute x0 -> x3, waiting for transfers between devices: none -> 139 us  [on_device(): lax.ppermute(by_rank[-1], axis_name='row', perm=[(w, (w + 1) % how_many)...]
    all_gather x1, waiting for transfers between devices: 32.8 us -> 0.01 us  [on_device(): own_rows = lax.all_gather(centered, 'col', axis=1, tiled=True)]
    all_to_all x1, waiting for transfers between devices: 127 us -> 94 us  [on_device(): lax.all_to_all(every_sample, 'col', split_axis=0, concat_axis=1, tiled=True)]
    dynamic_slice x0 -> x2, local copies, waits for them, and re-layouts: none -> 19.7 us  [on_device(): jnp.roll(s_next, (lax.axis_index('row') + 1) * centered.shape[0], axis=0)]
    unnamed x47 -> x60, local copies, waits for them, and re-layouts: 10.2 us -> 29.4 us
  transfers between devices with their start and end apart: 7 -> 9, of which waited for: 7 -> 8; matrix products, arithmetic and copies ran while one was open for 1% -> 6% of each run, Pallas kernels for 0% -> 0%
where the time goes in v1:
time: 943 us; the launch traced here: 936 us
  waiting for transfers between devices  462 us (49%)
  other arithmetic  249 us (26%)
  matrix products  93.4 us (10%)
  local copies, waits for them, and re-layouts  82 us (9%)
  blocking collectives  23.8 us (3%)
  between operations  20.2 us (2%)
    psum x4, waiting for transfers between devices, broadcast(): return lax.psum(block, axis)  229 us
    another operation x29, other arithmetic, on_device(): factor = jnp.linalg.cholesky(diag_block)  158 us
    ppermute x3, waiting for transfers between devices, on_device(): lax.ppermute(by_rank[-1], axis_name='row', perm=[(w, (w + 1) % how_many)...  139 us
    all_to_all x1, waiting for transfers between devices, on_device(): lax.all_to_all(every_sample, 'col', split_axis=0, concat_axis=1, tiled=True)  94 us
    another operation x5, other arithmetic, on_device(): lax.linalg.triangular_solve(factor, column, left_side=False, lower=True,...  79.2 us
    unnamed x60, local copies, waits for them, and re-layouts  29.4 us
    dot_general x2, matrix products, jacobian(): jnp.dot(embedded, weights[panel_index], precision=lax.Precision.HIGHEST,...  19.9 us
    dynamic_slice x2, local copies, waits for them, and re-layouts, on_device(): jnp.roll(s_next, (lax.axis_index('row') + 1) * centered.shape[0], axis=0)  19.7 us
  transfers between devices with their start and end apart: 9, of which 8 were waited for; matrix products, arithmetic and copies ran while one was open for 6% of the time, Pallas kernels for 0%

profile of v1, /device:TPU:0, one launch (start us, length us, event | category | flops | bytes accessed | tf_op | source)
XLA Modules:
  0.0 936.0 jit_solution(12710126732552718005)
XLA Ops:
  8.7 5.1 multiply_reduce_fusion
  13.9 12.8 %divide_multiply_fusion.1 = f32[1024,512]{0,1:T(8,128)S(1)} fusion(f32[2,1024,512]{2,1,0:T(8,128)} %param.19, f32[1024,1024]{0,1:T(8,128)} %get-tuple-element.138, f32[1024]{0:T(1024)S(1)} %add_rsqrt_fusion, f32[512]{0:T(512)S(1)} %bitcast.287, f32[512]{0:T(512)S(1)} %bitcast.286), kind=kOutput, calls=%fused_computation.19 | convolution fusion | flops 6446120960 | bytes 8396800 | tf_op jit(solution)/shard_map/dot_general | solution.py:34
  26.7 7.2 divide_multiply_fusion
  35.9 13.7 %all-reduce.3 = (f32[1024]{0:T(1024)S(1)}, f32[512,1]{0,1:T(1,128)S(1)}) all-reduce(f32[1024]{0:T(1024)S(1)} %fusion.4, f32[512,1]{0,1:T(1,128)S(1)} %bitcast.278), channel_id=1, replica_groups=mesh['row'=4,'col'=8] {'row'}, use_global_device_ids=true, to_apply=%region_2.0 | all-reduce | flops 1536 | bytes 12288 | tf_op jit(solution)/shard_map/psum | solution.py:53
  49.6 4.0 multiply_convert_fusion
  53.7 47.2 %collective-permute-done = bf16[1024,1024]{0,1:T(8,128)(2,1)S(1)} collective-permute-done((bf16[1024,1024]{0,1:T(8,128)(2,1)}, bf16[1024,1024]{0,1:T(8,128)(2,1)S(1)}, u32[]{:S(2)}, u32[]{:S(2)}) %collective-permute-start) | collective-permute-done | bytes 2097184 | tf_op jit(solution)/shard_map/ppermute | solution.py:62
  102.2 46.2 %collective-permute-done.1 = bf16[1024,1024]{0,1:T(8,128)(2,1)} collective-permute-done((bf16[1024,1024]{0,1:T(8,128)(2,1)S(1)}, bf16[1024,1024]{0,1:T(8,128)(2,1)}, u32[]{:S(2)}, u32[]{:S(2)}) %collective-permute-start.1) | collective-permute-done | bytes 2097184 | tf_op jit(solution)/shard_map/ppermute | solution.py:62
  148.4 45.6 %collective-permute-done.2 = bf16[1024,1024]{0,1:T(8,128)(2,1)} collective-permute-done((bf16[1024,1024]{0,1:T(8,128)(2,1)}, bf16[1024,1024]{0,1:T(8,128)(2,1)}, u32[]{:S(2)}, u32[]{:S(2)}) %collective-permute-start.2) | collective-permute-done | bytes 2097184 | tf_op jit(solution)/shard_map/ppermute | solution.py:62
  194.0 3.1 constant_dynamic-update-slice_fusion.7
  197.2 3.2 constant_dynamic-update-slice_fusion.6
  200.4 1.5 constant_dynamic-update-slice_fusion.5
  202.8 1.5 constant_dynamic-update-slice_fusion.4
  204.2 3.1 constant_dynamic-update-slice_fusion.3
  207.3 3.1 constant_dynamic-update-slice_fusion.2
  210.4 1.5 constant_dynamic-update-slice_fusion.1
  211.9 1.5 constant_dynamic-update-slice_fusion
  213.4 7.7 constant_dynamic-slice_fusion.2
  221.1 12.0 %copy.20 = bf16[4096,1024]{1,0:T(8,128)(2,1)} copy(bf16[4096,1024]{0,1:T(8,128)(2,1)} %constant_dynamic-slice_fusion.2) | data formatting | bytes 16777216 | tf_op jit(solution)/shard_map/jit(_roll_dynamic)/dynamic_slice | solution.py:69
  233.1 5.0 all-to-all-start
  238.2 94.0 %all-to-all-done = bf16[8,512,1024]{2,1,0:T(8,128)(2,1)} async-done(((bf16[8,512,1024]{2,1,0:T(8,128)(2,1)}), bf16[8,512,1024]{2,1,0:T(8,128)(2,1)}, u32[]{:S(2)}, u32[]{:S(2)}) %all-to-all-start) | async-done | bytes 8388640 | tf_op jit(solution)/shard_map/all_to_all | solution.py:70
  332.2 11.6 %copy.21 = bf16[512,8,1024]{0,2,1:T(8,128)(2,1)} copy(bf16[512,8,1024]{2,0,1:T(8,128)(2,1)} %bitcast.7) | data formatting | bytes 16777216 | tf_op jit(solution)/shard_map/all_to_all | solution.py:70
  343.8 15.9 %broadcast_select_fusion.1 = (f32[1024,512]{0,1:T(8,128)}, f32[1024,512]{0,1:T(8,128)S(1)}) fusion(pred[]{:T(512)S(6)} %eq.59, s32[512]{0:T(512)S(1)} %iota_add_fusion.1, s32[1024]{0:T(1024)S(1)} %iota_add_fusion, bf16[1024,8192]{0,1:T(8,128)(2,1)} %all-gather.2.cloned.1.call-done, bf16[512,8192]{0,1:T(8,128)(2,1)} %bitcast.263), kind=kOutput, calls=%fused_computation.117 | convolution fusion | flops 8592031744 | bytes 29366272 | tf_op jit(solution)/shard_map/dot_general | solution.py:71
  362.1 48.4 %all-reduce.9.cloned.1.call-done = f32[512,512]{0,1:T(8,128)} async-done(((f32[512,512]{0,1:T(8,128)}), f32[512,512]{0,1:T(8,128)}) %all-reduce.9.cloned.1.call-update) | async-done | bytes 1048592 | tf_op jit(solution)/shard_map/psum | solution.py:13
  410.5 2.3 broadcast_select_fusion.3
  412.9 70.2 %all-reduce.15.cloned.1.call-done = (f32[1024,512]{0,1:T(8,128)}, f32[512,512]{0,1:T(8,128)}) async-done(((f32[1024,512]{0,1:T(8,128)}, f32[512,512]{0,1:T(8,128)}), (f32[1024,512]{0,1:T(8,128)}, f32[512,512]{0,1:T(8,128)})) %all-reduce.15.cloned.1.call-update) | async-done | bytes 3145744 | tf_op jit(solution)/shard_map/psum | solution.py:13
  483.1 1.6 copy.23
  486.0 11.7 %cholesky.286 = f32[128,128]{1,0:T(8,128)S(1)} custom-call(f32[128,128]{1,0:T(8,128)S(1)} %cholesky.426), custom_call_target="Cholesky" | custom-call | tf_op jit(solution)/shard_map/jit(cholesky)/cholesky | solution.py:92
  497.9 9.8 %custom-call.35 = f32[1,128,128]{1,2,0:T(8,128)S(1)} custom-call(f32[1,128,128]{2,1,0:T(8,128)S(1)} %get-tuple-element.132), custom_call_target="InvertDiagBlocksLowerTriangular" | custom-call | tf_op jit(solution)/shard_map/jit(cholesky)/cholesky | solution.py:92
  510.2 11.7 %cholesky.305 = f32[128,128]{1,0:T(8,128)S(1)} custom-call(f32[128,128]{1,0:T(8,128)S(1)} %cholesky.430), custom_call_target="Cholesky" | custom-call | tf_op jit(solution)/shard_map/jit(cholesky)/cholesky | solution.py:92
  522.0 10.2 %custom-call.36 = f32[1,128,128]{1,2,0:T(8,128)S(1)} custom-call(f32[1,128,128]{2,1,0:T(8,128)S(1)} %get-tuple-element.129), custom_call_target="InvertDiagBlocksLowerTriangular" | custom-call | tf_op jit(solution)/shard_map/jit(cholesky)/cholesky | solution.py:92
  533.7 11.7 %cholesky.326 = f32[128,128]{1,0:T(8,128)S(1)} custom-call(f32[128,128]{1,0:T(8,128)S(1)} %cholesky.435), custom_call_target="Cholesky" | custom-call | tf_op jit(solution)/shard_map/jit(cholesky)/cholesky | solution.py:92
  546.2 9.8 %custom-call.37 = f32[1,128,128]{1,2,0:T(8,128)S(1)} custom-call(f32[1,128,128]{2,1,0:T(8,128)S(1)} %get-tuple-element.126), custom_call_target="InvertDiagBlocksLowerTriangular" | custom-call | tf_op jit(solution)/shard_map/jit(cholesky)/cholesky | solution.py:92
  557.4 11.7 %cholesky.343 = f32[128,128]{1,0:T(8,128)S(1)} custom-call(f32[128,128]{1,0:T(8,128)S(1)} %convolution_subtract_fusion.17), custom_call_target="Cholesky" | custom-call | tf_op jit(solution)/shard_map/jit(cholesky)/cholesky | solution.py:92
  573.4 8.2 while.14
  574.1 1.4 bitcast_dynamic-update-slice_fusion.4
  576.1 1.4 bitcast_dynamic-update-slice_fusion.4
  578.2 1.4 bitcast_dynamic-update-slice_fusion.4
  581.6 39.3 %custom-call.38 = f32[4,128,128]{1,2,0:T(8,128)S(1)} custom-call(f32[4,128,128]{2,1,0:T(8,128)S(1)} %get-tuple-element.72), custom_call_target="InvertDiagBlocksLowerTriangular" | custom-call | tf_op jit(solution)/shard_map/triangular_solve/custom-call.3 | solution.py:93
  621.0 1.7 fusion.85
  622.6 1.6 convolution_subtract_fusion.5
  624.9 1.8 convolution_subtract_fusion.3
  627.3 2.3 fusion.32
  633.1 1.5 convolution_subtract_fusion.11
  635.0 5.3 broadcast_select_fusion
  643.5 51.5 %all-reduce.11.cloned.1.call-done = f32[512,512]{0,1:T(8,128)} async-done(((f32[512,512]{0,1:T(8,128)}), f32[512,512]{0,1:T(8,128)}) %all-reduce.11.cloned.1.call-update) | async-done | bytes 1048592 | tf_op jit(solution)/shard_map/psum | solution.py:13
  698.3 10.1 %psum.71 = f32[512,1]{0,1:T(1,128)S(1)} all-reduce(f32[512,1]{0,1:T(1,128)S(1)} %bitcast.281), channel_id=1, replica_groups=mesh['row'=4,'col'=8] {'row'}, use_global_device_ids=true, to_apply=%region_18.23 | all-reduce | flops 512 | bytes 4096 | tf_op jit(solution)/shard_map/psum | solution.py:13
  708.5 58.9 %all-reduce.13.cloned.1.call-done = (f32[1024,512]{0,1:T(8,128)}, f32[512,512]{0,1:T(8,128)}) async-done(((f32[1024,512]{0,1:T(8,128)}, f32[512,512]{0,1:T(8,128)}), (f32[1024,512]{0,1:T(8,128)}, f32[512,512]{0,1:T(8,128)})) %all-reduce.13.cloned.1.call-update) | async-done | bytes 3145744 | tf_op jit(solution)/shard_map/psum | solution.py:13
  767.4 1.6 copy.28
  770.3 11.7 %cholesky.358 = f32[128,128]{1,0:T(8,128)S(1)} custom-call(f32[128,128]{1,0:T(8,128)S(1)} %cholesky.439), custom_call_target="Cholesky" | custom-call | tf_op jit(solution)/shard_map/jit(cholesky)/cholesky | solution.py:92
  782.2 9.8 %custom-call.40 = f32[1,128,128]{1,2,0:T(8,128)S(1)} custom-call(f32[1,128,128]{2,1,0:T(8,128)S(1)} %get-tuple-element.122), custom_call_target="InvertDiagBlocksLowerTriangular" | custom-call | tf_op jit(solution)/shard_map/jit(cholesky)/cholesky | solution.py:92
  794.5 11.7 %cholesky.377 = f32[128,128]{1,0:T(8,128)S(1)} custom-call(f32[128,128]{1,0:T(8,128)S(1)} %cholesky.443), custom_call_target="Cholesky" | custom-call | tf_op jit(solution)/shard_map/jit(cholesky)/cholesky | solution.py:92
  807.7 10.0 %custom-call.41 = f32[1,128,128]{1,2,0:T(8,128)S(1)} custom-call(f32[1,128,128]{2,1,0:T(8,128)S(1)} %get-tuple-element.119), custom_call_target="InvertDiagBlocksLowerTriangular" | custom-call | tf_op jit(solution)/shard_map/jit(cholesky)/cholesky | solution.py:92
  819.2 11.7 %cholesky.398 = f32[128,128]{1,0:T(8,128)S(1)} custom-call(f32[128,128]{1,0:T(8,128)S(1)} %cholesky.448), custom_call_target="Cholesky" | custom-call | tf_op jit(solution)/shard_map/jit(cholesky)/cholesky | solution.py:92
  831.6 9.8 %custom-call.42 = f32[1,128,128]{1,2,0:T(8,128)S(1)} custom-call(f32[1,128,128]{2,1,0:T(8,128)S(1)} %get-tuple-element.116), custom_call_target="InvertDiagBlocksLowerTriangular" | custom-call | tf_op jit(solution)/shard_map/jit(cholesky)/cholesky | solution.py:92
  842.8 11.7 %cholesky.415 = f32[128,128]{1,0:T(8,128)S(1)} custom-call(f32[128,128]{1,0:T(8,128)S(1)} %convolution_subtract_fusion.16), custom_call_target="Cholesky" | custom-call | tf_op jit(solution)/shard_map/jit(cholesky)/cholesky | solution.py:92
  858.1 8.2 while.15
  858.8 1.4 bitcast_dynamic-update-slice_fusion.5
  860.9 1.4 bitcast_dynamic-update-slice_fusion.5
  866.4 39.3 %custom-call.43 = f32[4,128,128]{1,2,0:T(8,128)S(1)} custom-call(f32[4,128,128]{2,1,0:T(8,128)S(1)} %get-tuple-element.74), custom_call_target="InvertDiagBlocksLowerTriangular" | custom-call | tf_op jit(solution)/shard_map/triangular_solve/custom-call.3 | solution.py:93
  907.1 1.7 fusion.83
  908.8 1.6 convolution_subtract_fusion.4
  918.4 1.5 convolution_subtract_fusion.10
  920.3 5.3 convolution_subtract_fusion
  925.6 2.9 copy.33
  (183 shorter events, 58.9 us)
Async XLA Ops:
  7.2 1.6 copy-start
  7.2 336.6 %all-gather.2.cloned.1.call-start = ((), (), s32[]{:S(2)}) async-start(), calls=%async_computation.1 | async-start | bytes 18874368 | tf_op jit(solution)/shard_map/all_gather | solution.py:57
  8.7 5.1 copy-start.22
  8.7 5.1 copy-start.23
  13.8 12.8 %copy-start.24 = (f32[2,1024,512]{2,1,0:T(8,128)S(1)}, f32[2,1024,512]{2,1,0:T(8,128)}, u32[]{:S(2)}) copy-start(f32[2,1024,512]{2,1,0:T(8,128)} %param.19) | copy-start | bytes 12582916
  13.9 12.8 %copy-start.25 = (f32[1024,1024]{0,1:T(8,128)S(1)}, f32[1024,1024]{0,1:T(8,128)}, u32[]{:S(2)}) copy-start(f32[1024,1024]{0,1:T(8,128)} %get-tuple-element.138) | copy-start | bytes 12582916
  26.6 7.2 copy-start.7
  33.9 1.3 copy-start.8
  35.2 0.7 copy-start.20
  53.6 47.3 %collective-permute-start = (bf16[1024,1024]{0,1:T(8,128)(2,1)}, bf16[1024,1024]{0,1:T(8,128)(2,1)S(1)}, u32[]{:S(2)}, u32[]{:S(2)}) collective-permute-start(bf16[1024,1024]{0,1:T(8,128)(2,1)} %multiply_convert_fusion), channel_id=1, source_target_pairs={{0,8},{8,16},{16,24},{24,0},{1,9},{9,17},{17,25},{25,1},{2,10},{10... | collective-permute-start | bytes 6291464 | tf_op jit(solution)/shard_map/ppermute | solution.py:62
  100.9 1.3 copy-start.5
  102.2 46.2 %collective-permute-start.1 = (bf16[1024,1024]{0,1:T(8,128)(2,1)S(1)}, bf16[1024,1024]{0,1:T(8,128)(2,1)}, u32[]{:S(2)}, u32[]{:S(2)}) collective-permute-start(bf16[1024,1024]{0,1:T(8,128)(2,1)S(1)} %collective-permute-done), channel_id=1, source_target_pairs={{0,8},{8,16},{16,24},{24,0},{1,9},{9,17},{17,25},{25,1},{2,10},{10... | collective-permute-start | bytes 6291464 | tf_op jit(solution)/shard_map/ppermute | solution.py:62
  148.4 45.6 %collective-permute-start.2 = (bf16[1024,1024]{0,1:T(8,128)(2,1)}, bf16[1024,1024]{0,1:T(8,128)(2,1)}, u32[]{:S(2)}, u32[]{:S(2)}) collective-permute-start(bf16[1024,1024]{0,1:T(8,128)(2,1)} %collective-permute-done.1), channel_id=1, source_target_pairs={{0,8},{8,16},{16,24},{24,0},{1,9},{9,17},{17,25},{25,1},{2,10},{10... | collective-permute-start | bytes 6291464 | tf_op jit(solution)/shard_map/ppermute | solution.py:62
  197.2 3.2 copy-start.6
  200.4 2.3 copy-start.2
  233.1 99.1 %all-to-all-start = ((bf16[8,512,1024]{2,1,0:T(8,128)(2,1)}), bf16[8,512,1024]{2,1,0:T(8,128)(2,1)}, u32[]{:S(2)}, u32[]{:S(2)}) async-start(bf16[8,512,1024]{2,1,0:T(8,128)(2,1)} %bitcast.254), calls=%async_computation | async-start | bytes 16777216 | tf_op jit(solution)/shard_map/all_to_all | solution.py:70
  238.2 172.4 %all-reduce.9.cloned.1.call-start = ((), (), s32[]{:S(2)}) async-start(), calls=%async_computation.2 | async-start | bytes 2097152 | tf_op jit(solution)/shard_map/psum | solution.py:13
  359.6 1.3 copy-start.9
  362.1 121.0 %all-reduce.15.cloned.1.call-start = ((), (), s32[]{:S(2)}) async-start(), calls=%async_computation.5 | async-start | bytes 6291456 | tf_op jit(solution)/shard_map/psum | solution.py:13
  412.8 282.1 %all-reduce.11.cloned.1.call-start = ((), (), s32[]{:S(2)}) async-start(), calls=%async_computation.3 | async-start | bytes 2097152 | tf_op jit(solution)/shard_map/psum | solution.py:13
  483.1 1.7 copy-start.12
  485.0 1.0 copy-start.16
  627.3 2.9 copy-start.14
  630.2 4.8 copy-start.17
  631.3 3.8 copy-start.10
  640.4 1.3 copy-start.3
  642.9 124.5 %all-reduce.13.cloned.1.call-start = ((), (), s32[]{:S(2)}) async-start(), calls=%async_computation.4 | async-start | bytes 6291456 | tf_op jit(solution)/shard_map/psum | solution.py:13
  696.1 1.0 copy-start.18
  767.4 1.7 copy-start.11
  769.3 1.0 copy-start.15
  906.4 4.7 copy-start.19
  913.6 1.8 copy-start.13
  916.5 3.8 copy-start.4
  920.3 8.8 copy-start.1
  928.5 0.6 copy-start.21
Sparse Core Ops, SparseCore 0:
  53.7 87.9 all-gather.1
  362.2 48.2 all-reduce.8
  414.4 68.6 all-reduce.14
  643.0 51.9 all-reduce.10
  698.7 68.6 all-reduce.12
